TPU v7x, 512 devices: a whole 4x4x16 slice. The times are simulated.
512 devices in a mesh: mem: 8 (over x, core), gx: 4 (over z_hi), gy: 16 (over z_lo, y).
Axes of the slice: x: 4, y: 4, z: 16 (z_hi: 4, z_lo: 4; z = z_hi * 4 + z_lo), core: 2. Of those that a mesh axis runs over, the one named last changes fastest.
Arguments:
- control: float32 [64, 3, 512, 512], P('mem', None, 'gy', 'gx'), may hold values from -6 to 6
- perturb: bfloat16 [64, 6, 3, 512, 512], P('mem', None, None, 'gy', 'gx'), may hold values from -6 to 6
- obs_count: int32 [3, 512, 512], P(None, 'gy', 'gx'), may hold values from 0 to 3
- obs_weight: float32 [6], replicated, may hold values from 0.3 to 3
- diffusivity: float32 [3, 512, 512], P(None, 'gy', 'gx'), may hold values from 0.12 to 0.24
Outputs:
- hess_product: float32 [64, 3, 512, 512], P('mem', None, 'gy', 'gx')
All inputs are finite; a program needn't handle non-finite values.
Results may differ from a plain program's by a relative error of at most 0.0003.
Values sent between devices are 32-bit elements; how exact they have to be, the bound alone decides.
No kernel may reach another device: no remote copies, remote signals or barrier semaphores. Data moves between devices by JAX's collectives and lax.ppermute only.
A program may use at most 64 MiB of HBM per device.

v0:
```python
import math

import jax
import jax.numpy as jnp
from jax import lax
from jax.experimental import pallas as pl
from jax.experimental.pallas import tpu as pltpu
from jax.sharding import PartitionSpec as P


STEPS = 4
LANES = 128
SUBLANES = 8
PARAMS = pltpu.CompilerParams(vmem_limit_bytes=16 << 20)


def swap(near, far, axis):
    size = lax.axis_size(axis)
    out = []
    for value, start in ((near, 0), (far, 1)):
        pairs = []
        for i in range(start, size - 1, 2):
            pairs += [(i, i + 1), (i + 1, i)]
        out.append(lax.ppermute(value, axis, pairs))
    return out


def is_odd(axis):
    return lax.rem(lax.axis_index(axis), 2) == 1


def ordered(odd, first, last):
    return jnp.where(odd, first, last), jnp.where(odd, last, first)


class Grid:
    def __init__(self, members, levels, rows):
        self.members, self.levels, self.rows = members, levels, rows
        self.wide = rows + 4 * STEPS
        self.ring = rows + 2 * STEPS
        self.block = LANES // levels // STEPS * STEPS
        self.per = self.block // STEPS
        self.wide_packs = -(-self.wide // self.per)
        self.packs = -(-self.ring // self.per)
        self.padded = self.per * SUBLANES

    def members_at(self, level, y):
        return pl.ds(level * self.rows + y, self.members, stride=self.levels * self.rows)

    def rim_at(self, level, r):
        return pl.ds(level * self.members * STEPS + r, self.members, stride=STEPS)

    def wide_row(self, field, got, odd, level, k):
        y = k - 2 * STEPS
        if 0 <= y < self.rows:
            return field[self.members_at(level, y), :]
        before = y < 0
        at = level * 2 * STEPS + (k if before else y - self.rows)
        near, far = got
        after_value, before_value = ordered(odd, far[at], near[at])
        return before_value if before else after_value

    def ring_row(self, field, before, after, level, k):
        y = k - STEPS
        if y < 0:
            return before[self.rim_at(level, k), :]
        if y >= self.rows:
            return after[self.rim_at(level, y - self.rows), :]
        return field[self.members_at(level, y), :]

    def set_ring_row(self, field, before, after, level, k, value):
        y = k - STEPS
        if y < 0:
            before[self.rim_at(level, k), :] = value
        elif y >= self.rows:
            after[self.rim_at(level, y - self.rows), :] = value
        else:
            field[self.members_at(level, y), :] = value

    def tile_of(self, ref, plane, j):
        t = plane * (self.ring // SUBLANES) + j
        return t // (ref.shape[1] // SUBLANES), pl.ds(t % (ref.shape[1] // SUBLANES) * SUBLANES, SUBLANES)

    def lanes(self, rows=SUBLANES):
        lane = lax.broadcasted_iota(jnp.int32, (rows, LANES), 1)
        return lax.rem(lane, self.block)


def within(place, start, size):
    return (place >= start) & (place < start + size)


def rolled(value, shift):
    shift %= LANES
    return pltpu.roll(value, shift, 1) if shift else value


def edges_of(grid, value_of, rows=SUBLANES):
    lane = lax.broadcasted_iota(jnp.int32, (rows, LANES), 1)
    out = jnp.zeros((rows, LANES), jnp.float32)
    for l in range(grid.levels):
        base = l * grid.block
        out = jnp.where(within(lane, base, 4 * STEPS), rolled(value_of(l), base + 2 * STEPS), out)
    return out


def packed(grid, edges, rows=SUBLANES):
    place = grid.lanes(rows)
    first = jnp.zeros((rows, LANES), jnp.float32)
    last = first
    for i, value in enumerate(edges):
        mask = within(place, i * STEPS, STEPS)
        first = jnp.where(mask, rolled(value, (i - 2) * STEPS), first)
        last = jnp.where(mask, rolled(value, (i - 1) * STEPS), last)
    return first, last


def strip_of(grid, edges, west, east, i, rows=SUBLANES):
    place = grid.lanes(rows)
    out = jnp.where(place < 2 * STEPS, edges, 0.0)
    out = jnp.where(within(place, 6 * STEPS, 2 * STEPS), rolled(edges, 4 * STEPS), out)
    out = jnp.where(within(place, 2 * STEPS, STEPS), rolled(east, (2 - i) * STEPS), out)
    return jnp.where(within(place, 5 * STEPS, STEPS), rolled(west, (5 - i) * STEPS), out)


def joined(grid, strip):
    return jnp.where(grid.lanes() < 2 * STEPS, strip, rolled(strip, -4 * STEPS))


def merged(grid, main, ends, level):
    lane = lax.broadcasted_iota(jnp.int32, main.shape, 1)
    outer = (lane < STEPS) | (lane >= LANES - STEPS)
    return jnp.where(outer, rolled(ends, LANES - 2 * STEPS - level * grid.block), main)


def lateral(value):
    return pltpu.roll(value, 1, 1) + pltpu.roll(value, LANES - 1, 1)


def spread_steps(field, coef, keep):
    for s in range(1, STEPS + 1):
        new = list(field)
        for k in range(s, len(field) - s):
            around = (field[k - 1] + field[k + 1]) + lateral(field[k])
            new[k] = keep(k) * field[k] + coef(k) * around
        field = new
    return field[STEPS:-STEPS]


def adjoint_steps(field, coef, keep):
    for s in range(1, STEPS + 1):
        flux = {k: coef(k) * field[k] for k in range(s - 1, len(field) - s + 1)}
        new = list(field)
        for k in range(s, len(field) - s):
            new[k] = keep(k) * field[k] + ((flux[k - 1] + flux[k + 1]) + lateral(flux[k]))
        field = new
    return field[STEPS:-STEPS]


def row_reader(ref, start):
    return lambda k: jnp.broadcast_to(ref[pl.ds(start + k, 1), :], (SUBLANES, LANES))


def turned(value):
    return pltpu.roll(value, STEPS, 0)


def upper():
    return lax.broadcasted_iota(jnp.int32, (SUBLANES, LANES), 0) < STEPS


def rows_kernel(
    grid,
    control_hbm,
    diffusivity_hbm,
    count_hbm,
    weight_hbm,
    perturb_hbm,
    near,
    far,
    outer_near,
    outer_far,
    control,
    diffusivity,
    seen,
    weights,
    count,
    weight,
    heads,
    tails,
    sems,
):
    levels, rows = grid.levels, grid.rows
    depth = 2 * STEPS
    pairs = (
        (diffusivity_hbm, diffusivity),
        (count_hbm, count),
        (weight_hbm, weight),
        (control_hbm, control),
        (perturb_hbm.at[:, :, :, pl.ds(0, SUBLANES), :], heads),
        (perturb_hbm.at[:, :, :, pl.ds(rows - SUBLANES, SUBLANES), :], tails),
    )
    copies = [pltpu.make_async_copy(source, target, sems.at[i]) for i, (source, target) in enumerate(pairs)]
    for copy in copies:
        copy.start()
    odd = is_odd("gy")
    for copy in copies[:3]:
        copy.wait()
    for v in range(weights.shape[0]):
        weights[v] = jnp.full((SUBLANES, LANES), weight[v])
    seen[...] = count[...].astype(jnp.float32)
    at = levels * depth
    for l in range(levels):
        first = diffusivity[l * rows : l * rows + depth, :]
        last = diffusivity[(l + 1) * rows - depth : (l + 1) * rows, :]
        near[at + l], far[at + l] = ordered(odd, first, last)
        first = seen[l * rows : l * rows + STEPS, :]
        last = seen[(l + 1) * rows - STEPS : (l + 1) * rows, :]
        slot, sub = divmod(l * STEPS, SUBLANES)
        a, b = ordered(odd, first, last)
        near[at + levels + slot, sub : sub + STEPS, :] = a
        far[at + levels + slot, sub : sub + STEPS, :] = b
    copies[3].wait()
    for l in range(levels):
        for r in range(depth):
            first = control[grid.members_at(l, r), :]
            last = control[grid.members_at(l, rows - depth + r), :]
            near[l * depth + r], far[l * depth + r] = ordered(odd, first, last)
    copies[4].wait()
    copies[5].wait()
    members, variables = heads.shape[:2]
    for q in range(members // 2):
        for v in range(variables):
            for l in range(levels):
                head = [heads[2 * q + j, v, l].astype(jnp.float32) for j in range(2)]
                tail = [tails[2 * q + j, v, l].astype(jnp.float32) for j in range(2)]
                first = jnp.where(upper(), head[0], turned(head[1]))
                last = jnp.where(upper(), turned(tail[0]), tail[1])
                at = (v * levels + l) * (members // 2) + q
                outer_near[at], outer_far[at] = ordered(odd, first, last)


def field_columns(grid, row_of, length, near, far, edges):
    for start in range(0, length, grid.per):
        here = []
        for k in range(start, min(length, start + grid.per)):
            here.append(edges_of(grid, lambda l: row_of(l, k)))
            edges[k] = here[-1]
        q = start // grid.per
        near[q], far[q] = ordered(is_odd("gx"), *packed(grid, here))


def columns_kernel(grid, control, diffusivity, got_near, got_far, near, far, edges, ring, ring_edges):
    got = (got_near, got_far)
    odd = is_odd("gy")
    field_columns(grid, lambda l, k: grid.wide_row(control, got, odd, l, k), grid.wide, near, far, edges)
    depth = 2 * STEPS
    for l in range(grid.levels):
        after, before = ordered(odd, got_far[grid.levels * depth + l], got_near[grid.levels * depth + l])
        base = l * grid.wide
        ring[base : base + depth, :] = before
        ring[base + depth : base + depth + grid.rows, :] = diffusivity[l * grid.rows : (l + 1) * grid.rows, :]
        ring[base + depth + grid.rows : base + grid.wide, :] = after
    ring_edges[...] = jnp.zeros(ring_edges.shape, jnp.float32)
    ring_edges[: grid.wide, :] = edges_of(grid, lambda l: ring[l * grid.wide : (l + 1) * grid.wide, :], grid.wide)
    packs = grid.wide_packs
    spaced = [ring_edges[pl.ds(i, packs, stride=grid.per), :] for i in range(grid.per)]
    a, b = ordered(is_odd("gx"), *packed(grid, spaced, packs))
    near[packs, :packs, :] = a
    far[packs, :packs, :] = b


def spread_main_kernel(grid, control, ring, got_near, got_far, perturb_hbm, main, main_before, main_after, perturb, keep, sem):
    copy = pltpu.make_async_copy(perturb_hbm, perturb, sem)
    copy.start()
    odd = is_odd("gy")
    keep[...] = 1.0 - 4.0 * ring[...]
    for l in range(grid.levels):
        rows = [grid.wide_row(control, (got_near, got_far), odd, l, k) for k in range(grid.wide)]
        at = l * grid.wide
        for k, row in enumerate(spread_steps(rows, row_reader(ring, at), row_reader(keep, at))):
            grid.set_ring_row(main, main_before, main_after, l, k, row)
    copy.wait()


def adjoint_main_kernel(grid, back, before, after, ring, main, keep):
    keep[...] = 1.0 - 4.0 * ring[...]
    for l in range(grid.levels):
        rows = [grid.ring_row(back, before, after, l, k) for k in range(grid.ring)]
        at = l * grid.wide + STEPS
        for y, row in enumerate(adjoint_steps(rows, row_reader(ring, at), row_reader(keep, at))):
            main[grid.members_at(l, y), :] = row


def sides(col_near, col_far, q):
    east, west = ordered(is_odd("gx"), col_far[q], col_near[q])
    return west, east


def strip_steps(grid, steps, edges, length, skip, col_near, col_far, strip_ring, strip_keep):
    strip_keep[...] = 1.0 - 4.0 * strip_ring[...]
    field = []
    for k in range(length):
        q, i = divmod(k, grid.per)
        field.append(strip_of(grid, edges[k], *sides(col_near, col_far, q), i))
    return [joined(grid, strip) for strip in steps(field, row_reader(strip_ring, skip), row_reader(strip_keep, skip))]


def spread_kernel(
    grid,
    main,
    main_before,
    main_after,
    edges,
    ring_edges,
    col_near,
    col_far,
    perturb,
    rim_near,
    rim_far,
    partial,
    strip_ring,
    strip_keep,
    ends,
    ends_before,
    ends_after,
):
    packs = grid.wide_packs
    west, east = (side[:packs] for side in sides(col_near, col_far, packs))
    strip_ring[...] = jnp.zeros(strip_ring.shape, jnp.float32)
    for i in range(grid.per):
        at = pl.ds(i, packs, stride=grid.per)
        strip_ring[at, :] = strip_of(grid, ring_edges[at, :], west, east, i, packs)
    members, variables, levels, rows, _ = perturb.shape
    one = Grid(members, 1, rows)
    for k, value in enumerate(strip_steps(grid, spread_steps, edges, grid.wide, 0, col_near, col_far, strip_ring, strip_keep)):
        one.set_ring_row(ends, ends_before, ends_after, 0, k, value)
    tile = 2 * SUBLANES
    odd = is_odd("gy")
    pairs = members // 2
    for l in range(levels):
        for start in range(0, rows, tile):
            here = []
            for m in range(members):
                at = pl.ds((m * levels + l) * rows + start, tile)
                here.append(merged(grid, main[at, :], ends[pl.ds(m * rows + start, tile), :], l))
            for v in range(variables):
                total = perturb[0, v, l, start : start + tile, :].astype(jnp.float32) * here[0]
                for m in range(1, members):
                    total = total + perturb[m, v, l, start : start + tile, :].astype(jnp.float32) * here[m]
                for j in range(2):
                    partial[grid.tile_of(partial, v * levels + l, start // SUBLANES + j)] = total[j * SUBLANES : (j + 1) * SUBLANES]
        rims = []
        for q in range(pairs):
            at, end_at = pl.ds((l * pairs + q) * SUBLANES, SUBLANES), pl.ds(q * SUBLANES, SUBLANES)
            both = ((main_after, ends_after), (main_before, ends_before))
            rims.append([merged(grid, m[at, :], e[end_at, :], l) for m, e in both])
        for v in range(variables):
            totals = [0.0, 0.0]
            for q in range(pairs):
                at = (v * levels + l) * pairs + q
                outer = ordered(odd, rim_far[at], rim_near[at])
                totals = [t + p * r for t, p, r in zip(totals, outer, rims[q])]
            after, before = (t + turned(t) for t in totals)
            partial[grid.tile_of(partial, v * levels + l, rows // SUBLANES)] = jnp.where(upper(), after, before)
    used = variables * levels * (grid.ring // SUBLANES)
    for t in range(used, partial.shape[0] * partial.shape[1] // SUBLANES):
        partial[grid.tile_of(partial, 0, t)] = jnp.zeros((SUBLANES, LANES), jnp.float32)


def back_kernel(
    grid,
    scale,
    increment,
    seen,
    weights,
    perturb,
    rim_near,
    rim_far,
    got_near,
    got_far,
    back,
    back_before,
    back_after,
    edges,
    near,
    far,
):
    members, variables, levels, rows, _ = perturb.shape
    tile = 2 * SUBLANES
    odd = is_odd("gy")
    pairs = members // 2
    for l in range(levels):
        for start in range(0, rows, tile):
            factor = seen[l * rows + start : l * rows + start + tile, :] * (scale * scale)
            weighted = []
            for v in range(variables):
                at = [grid.tile_of(increment, v * levels + l, start // SUBLANES + j) for j in range(2)]
                pair = [weights[v] * increment[a] for a in at]
                weighted.append(factor * jnp.concatenate(pair, axis=0))
            for m in range(members):
                total = perturb[m, 0, l, start : start + tile, :].astype(jnp.float32) * weighted[0]
                for v in range(1, variables):
                    total = total + perturb[m, v, l, start : start + tile, :].astype(jnp.float32) * weighted[v]
                base = (m * levels + l) * rows
                back[base + start : base + start + tile, :] = total
        slot, sub = divmod(l * STEPS, SUBLANES)
        slot += levels * 2 * STEPS + levels
        counts = ordered(odd, got_far[slot, sub : sub + STEPS, :], got_near[slot, sub : sub + STEPS, :])
        counts = [jnp.concatenate([c, c], axis=0) * (scale * scale) for c in counts]
        totals = [[0.0] * pairs, [0.0] * pairs]
        for v in range(variables):
            both = increment[grid.tile_of(increment, v * levels + l, rows // SUBLANES)]
            after = jnp.where(upper(), both, turned(both))
            before = jnp.where(upper(), turned(both), both)
            weighted = [c * (weights[v] * w) for c, w in zip(counts, (after, before))]
            for q in range(pairs):
                at = (v * levels + l) * pairs + q
                for side, p in enumerate(ordered(odd, rim_far[at], rim_near[at])):
                    totals[side][q] = totals[side][q] + p * weighted[side]
        for q in range(pairs):
            at = slice((l * pairs + q) * SUBLANES, (l * pairs + q + 1) * SUBLANES)
            back_after[at, :] = totals[0][q]
            back_before[at, :] = totals[1][q]
    field_columns(grid, lambda l, k: grid.ring_row(back, back_before, back_after, l, k), grid.ring, near, far, edges)


def adjoint_kernel(grid, control, main, edges, strip_ring, col_near, col_far, out_hbm, strip_keep, ends, out, sems):
    results = strip_steps(grid, adjoint_steps, edges, grid.ring, STEPS, col_near, col_far, strip_ring, strip_keep)
    for y, value in enumerate(results):
        ends[pl.ds(y, grid.members, stride=grid.rows), :] = value
    planes = (grid.members * grid.levels, grid.rows, LANES)
    copies = []
    for start in range(0, grid.rows, SUBLANES):
        for m in range(grid.members):
            end = ends[pl.ds(m * grid.rows + start, SUBLANES), :]
            for l in range(grid.levels):
                at = pl.ds((m * grid.levels + l) * grid.rows + start, SUBLANES)
                out[at, :] = control[at, :] + merged(grid, main[at, :], end, l)
        part = pl.ds(start, SUBLANES)
        copies.append(pltpu.make_async_copy(out.reshape(planes).at[:, part, :], out_hbm.at[:, part, :], sems.at[start // SUBLANES]))
        copies[-1].start()
    for copy in copies:
        copy.wait()


def shape_of(*shape):
    return jax.ShapeDtypeStruct(shape, jnp.float32)


def shards(control, perturb, obs_count, obs_weight, diffusivity):
    members, levels, rows, lanes = control.shape
    variables = perturb.shape[1]
    ways = lax.axis_size("mem")
    scale = 1.0 / math.sqrt(members * ways - 1)
    count = members * levels
    grid = Grid(members, levels, rows)
    assert members == SUBLANES and lanes == LANES and grid.block >= 8 * STEPS
    vmem = pl.BlockSpec(memory_space=pltpu.VMEM)
    hbm = pl.BlockSpec(memory_space=pltpu.HBM)
    f32 = jnp.float32

    def call(kernel, *args, work=0, **kwargs):
        cost = pl.CostEstimate(flops=work, bytes_accessed=work, transcendentals=0) if work else None
        return pl.pallas_call(
            lambda *refs: kernel(grid, *refs), compiler_params=PARAMS, cost_estimate=cost, **kwargs
        )(*args)

    def in_hbm(array):
        return pltpu.with_memory_space_constraint(array, pltpu.HBM)

    depth = 2 * STEPS
    ring_shape, strip_shape = (levels * grid.wide, lanes), (grid.padded, lanes)
    rim = shape_of(count * STEPS, lanes)

    def tiles(number):
        return shape_of(number, SUBLANES, lanes)

    edge = tiles(levels * depth + levels + -(-levels * STEPS // SUBLANES))
    outer = tiles(variables * levels * members // 2)
    level_rows = shape_of(levels * rows, lanes)
    edge_rows = pltpu.VMEM((members, variables, levels, SUBLANES, lanes), perturb.dtype)
    near, far, outer_near, outer_far, flat, flat_diff, seen, weights = call(
        rows_kernel,
        in_hbm(control.reshape(count * rows, lanes)),
        in_hbm(diffusivity.reshape(levels * rows, lanes)),
        in_hbm(obs_count.reshape(levels * rows, lanes)),
        in_hbm(obs_weight),
        in_hbm(perturb),
        out_shape=(edge, edge, outer, outer, shape_of(count * rows, lanes), level_rows, level_rows, tiles(variables)),
        in_specs=[hbm] * 5,
        scratch_shapes=[
            pltpu.VMEM(level_rows.shape, jnp.int32),
            pltpu.SMEM(obs_weight.shape, f32),
            edge_rows,
            edge_rows,
            pltpu.SemaphoreType.DMA((6,)),
        ],
    )
    got = swap(near, far, "gy")
    rims = swap(outer_near, outer_far, "gy")
    edge = tiles(grid.wide_packs + 1)
    near, far, edges, ring, ring_edges = call(
        columns_kernel,
        flat,
        flat_diff,
        *got,
        out_shape=(edge, edge, tiles(grid.wide), shape_of(*ring_shape), shape_of(*strip_shape)),
    )
    sides = swap(near, far, "gx")
    *main, held = call(
        spread_main_kernel,
        flat,
        ring,
        *got,
        in_hbm(perturb),
        work=6 << 20,
        out_shape=(shape_of(count * rows, lanes), rim, rim, jax.ShapeDtypeStruct(perturb.shape, perturb.dtype)),
        in_specs=[vmem] * 4 + [hbm],
        scratch_shapes=[pltpu.VMEM(ring_shape, f32), pltpu.SemaphoreType.DMA],
    )
    piece = -(-variables * levels * grid.ring // (ways * SUBLANES)) * SUBLANES
    partial, strip_ring = call(
        spread_kernel,
        *main,
        edges,
        ring_edges,
        *sides,
        held,
        *rims,
        out_shape=(shape_of(ways, piece, lanes), shape_of(*strip_shape)),
        scratch_shapes=[
            pltpu.VMEM(strip_shape, f32),
            pltpu.VMEM((members * rows, lanes), f32),
            pltpu.VMEM((members * STEPS, lanes), f32),
            pltpu.VMEM((members * STEPS, lanes), f32),
        ],
    )

    parts = lax.all_to_all(partial, "mem", 0, 0)
    mine = jnp.sum(parts, axis=0)
    increment = lax.all_to_all(jnp.broadcast_to(mine, parts.shape), "mem", 0, 0)

    edge = tiles(grid.packs)
    back, before, after, edges, near, far = call(
        lambda grid, *refs: back_kernel(grid, scale, *refs),
        increment,
        seen,
        weights,
        held,
        *rims,
        *got,
        out_shape=(shape_of(count * rows, lanes), rim, rim, tiles(grid.ring), edge, edge),
    )
    sides = swap(near, far, "gx")
    main = call(
        adjoint_main_kernel,
        back,
        before,
        after,
        ring,
        work=6 << 20,
        out_shape=shape_of(count * rows, lanes),
        scratch_shapes=[pltpu.VMEM(ring_shape, f32)],
    )
    out = call(
        adjoint_kernel,
        flat,
        main,
        edges,
        strip_ring,
        *sides,
        out_shape=shape_of(count, rows, lanes),
        out_specs=hbm,
        scratch_shapes=[
            pltpu.VMEM(strip_shape, f32),
            pltpu.VMEM((members * rows, lanes), f32),
            pltpu.VMEM((count * rows, lanes), f32),
            pltpu.SemaphoreType.DMA((rows // SUBLANES,)),
        ],
    )
    return out.reshape(control.shape)


def solution(mesh):
    placed = (
        P("mem", None, "gy", "gx"),
        P("mem", None, None, "gy", "gx"),
        P(None, "gy", "gx"),
        P(),
        P(None, "gy", "gx"),
    )

    return jax.shard_map(shards, mesh=mesh, in_specs=placed, out_specs=P("mem", None, "gy", "gx"), check_vma=False)
```

profile of v0, /device:TPU:24, one launch (start us, length us, event | category | flops | bytes accessed | tf_op | source)
XLA Modules:
  0.0 73.4 jit_solution(3638772254882557810)
XLA Ops:
  0.0 1.4 %shard_map.55 = (f32[29,8,128]{2,1,0:T(8,128)S(1)}, f32[29,8,128]{2,1,0:T(8,128)S(1)}, f32[72,8,128]{2,1,0:T(8,128)S(1)}, f32[72,8,128]{2,1,0:T(8,128)S(1)}, f32...) custom-call(f32[768,128]{1,0:T(8,128)} %bitcast.4, ...), custom_call_target="tpu_custom_call" | custom-call | tf_op jit(solution)/shard_map/pallas_call | solution.py:465
  1.4 2.7 %collective-permute-start.4 = (f32[72,8,128]{2,1,0:T(8,128)S(1)}, f32[72,8,128]{2,1,0:T(8,128)S(1)}, u32[]{:S(2)}, u32[]{:S(2)}) collective-permute-start(f32[72,8,128]{2,1,0:T(8,128)S(1)} %get-tuple-element.43), channel_id=1, source_target_pairs={{0,1},{1,0},{2,3},{3,2},{4,5},{5,4},{6,7},{7,6},{8,9},{9,8},{10,11... | collective-permute-start | bytes 884744 | tf_op jit(solution)/shard_map/ppermute | solution.py:24
  4.1 4.3 %collective-permute-start.5 = (f32[72,8,128]{2,1,0:T(8,128)S(1)}, f32[72,8,128]{2,1,0:T(8,128)S(1)}, u32[]{:S(2)}, u32[]{:S(2)}) collective-permute-start(f32[72,8,128]{2,1,0:T(8,128)S(1)} %get-tuple-element.44), channel_id=1, source_target_pairs={{1,2},{2,1},{3,4},{4,3},{5,6},{6,5},{7,8},{8,7},{9,10},{10,9},{11,... | collective-permute-start | bytes 884744 | tf_op jit(solution)/shard_map/ppermute | solution.py:24
  8.4 5.7 %collective-permute-start = (f32[29,8,128]{2,1,0:T(8,128)S(1)}, f32[29,8,128]{2,1,0:T(8,128)S(1)}, u32[]{:S(2)}, u32[]{:S(2)}) collective-permute-start(f32[29,8,128]{2,1,0:T(8,128)S(1)} %get-tuple-element.32), channel_id=1, source_target_pairs={{0,1},{1,0},{2,3},{3,2},{4,5},{5,4},{6,7},{7,6},{8,9},{9,8},{10,11... | collective-permute-start | bytes 356360 | tf_op jit(solution)/shard_map/ppermute | solution.py:24
  14.1 1.9 %collective-permute-start.1 = (f32[29,8,128]{2,1,0:T(8,128)S(1)}, f32[29,8,128]{2,1,0:T(8,128)S(1)}, u32[]{:S(2)}, u32[]{:S(2)}) collective-permute-start(f32[29,8,128]{2,1,0:T(8,128)S(1)} %get-tuple-element.33), channel_id=1, source_target_pairs={{1,2},{2,1},{3,4},{4,3},{5,6},{6,5},{7,8},{8,7},{9,10},{10,9},{11,... | collective-permute-start | bytes 356360 | tf_op jit(solution)/shard_map/ppermute | solution.py:24
  16.1 0.9 %collective-permute-done.refs_2_.refs_6_ = f32[29,8,128]{2,1,0:T(8,128)S(1)} collective-permute-done((f32[29,8,128]{2,1,0:T(8,128)S(1)}, f32[29,8,128]{2,1,0:T(8,128)S(1)}, u32[]{:S(2)}, u32[]{:S(2)}) %collective-permute-start) | collective-permute-done | bytes 118816 | tf_op jit(solution)/shard_map/ppermute | solution.py:24
  16.9 6.0 %collective-permute-done.1.refs_3_.refs_7_ = f32[29,8,128]{2,1,0:T(8,128)S(1)} collective-permute-done((f32[29,8,128]{2,1,0:T(8,128)S(1)}, f32[29,8,128]{2,1,0:T(8,128)S(1)}, u32[]{:S(2)}, u32[]{:S(2)}) %collective-permute-start.1) | collective-permute-done | bytes 118816 | tf_op jit(solution)/shard_map/ppermute | solution.py:24
  23.0 0.6 shard_map.56
  23.5 5.3 %collective-permute-start.2 = (f32[6,8,128]{2,1,0:T(8,128)S(1)}, f32[6,8,128]{2,1,0:T(8,128)S(1)}, u32[]{:S(2)}, u32[]{:S(2)}) collective-permute-start(f32[6,8,128]{2,1,0:T(8,128)S(1)} %get-tuple-element.40), channel_id=1, source_target_pairs={{0,16},{16,0},{32,48},{48,32},{1,17},{17,1},{33,49},{49,33},{2,18}... | collective-permute-start | bytes 73736 | tf_op jit(solution)/shard_map/ppermute | solution.py:24
  28.8 0.7 collective-permute-start.3
  29.5 1.4 %shard_map.57 = (f32[768,128]{1,0:T(8,128)S(1)}, f32[96,128]{1,0:T(8,128)S(1)}, f32[96,128]{1,0:T(8,128)S(1)}, bf16[8,6,3,32,128]{4,3,2,1,0:T(8,128)(2,1)S(1)}) custom-call(f32[768,128]{1,0:T(8,128)S(1)} %get-tuple-element.30.refs_0_, f32[144,128]{1,0:T(8,128)S(1)} %get-tuple-element.34.refs_1_.refs_3_, ...), custom_call_target="tpu_custom_call" | custom-call | flops 6291456 | bytes 6291456 | tf_op jit(solution)/shard_map/pallas_call | solution.py:465
  30.9 2.5 %collective-permute-done.2.refs_5_ = f32[6,8,128]{2,1,0:T(8,128)S(1)} collective-permute-done((f32[6,8,128]{2,1,0:T(8,128)S(1)}, f32[6,8,128]{2,1,0:T(8,128)S(1)}, u32[]{:S(2)}, u32[]{:S(2)}) %collective-permute-start.2) | collective-permute-done | bytes 24608 | tf_op jit(solution)/shard_map/ppermute | solution.py:24
  33.4 0.0 collective-permute-done.3.refs_6_
  33.4 0.0 collective-permute-done.4.refs_8_.refs_4_
  33.4 0.0 collective-permute-done.5.refs_9_.refs_5_
  33.4 1.1 %shard_map.58 = (f32[8,96,128]{2,1,0:T(8,128)S(1)}, f32[80,128]{1,0:T(8,128)S(1)}) custom-call(f32[768,128]{1,0:T(8,128)S(1)} %get-tuple-element.35.refs_0_, f32[96,128]{1,0:T(8,128)S(1)} %get-tuple-element.36.refs_1_, f32[96,128]{1,0:T(8,128)S(1)} %get-tuple-element.37.refs_2_, f32[48,8,128]{2,1,0:T(8,128)S(1)} %get-tuple-element.38.refs_3_, ...), custom_call_target="tpu_custom_call" | custom-call | tf_op jit(solution)/shard_map/pallas_call | solution.py:465
  34.5 11.3 %all_to_all.10 = f32[8,96,128]{2,1,0:T(8,128)S(1)} all-to-all(f32[8,96,128]{2,1,0:T(8,128)S(1)} %get-tuple-element.45), channel_id=1, replica_groups=mesh['mem'=8,'gx'=4,'gy'=16] {'mem'}, dimensions={0} | all-to-all | bytes 786432 | tf_op jit(solution)/shard_map/all_to_all | solution.py:540
  45.9 11.3 %all_to_all.11.refs_0_ = f32[8,96,128]{2,1,0:T(8,128)S(1)} all-to-all(f32[8,96,128]{2,1,0:T(8,128)S(1)} %broadcast_in_dim.3), channel_id=1, replica_groups=mesh['mem'=8,'gx'=4,'gy'=16] {'mem'}, dimensions={0} | all-to-all | bytes 786432 | tf_op jit(solution)/shard_map/all_to_all | solution.py:542
  57.2 0.8 %shard_map.59 = (f32[768,128]{1,0:T(8,128)S(1)}, f32[96,128]{1,0:T(8,128)S(1)}, f32[96,128]{1,0:T(8,128)S(1)}, f32[40,8,128]{2,1,0:T(8,128)S(1)}, f32[4,8,128]{2,1,0:T(8,128)S(1)}, /*index=5*/f32[4,8,128]{2,1,0:T(8,128)S(1)}) custom-call(f32[8,96,128]{2,1,0:T(8,128)S(1)} %all_to_all.11.refs_0_, f32[96,128]{1,0:T(8,128)S(1)} %get-tuple-element.46.refs_1_, ...), custom_call_target="tpu_custom_call" | custom-call | tf_op jit(solution)/shard_map/pallas_call | solution.py:465
  57.9 12.2 %collective-permute-start.6 = (f32[4,8,128]{2,1,0:T(8,128)S(1)}, f32[4,8,128]{2,1,0:T(8,128)S(1)}, u32[]{:S(2)}, u32[]{:S(2)}) collective-permute-start(f32[4,8,128]{2,1,0:T(8,128)S(1)} %get-tuple-element.53), channel_id=1, source_target_pairs={{0,16},{16,0},{32,48},{48,32},{1,17},{17,1},{33,49},{49,33},{2,18}... | collective-permute-start | bytes 49160 | tf_op jit(solution)/shard_map/ppermute | solution.py:24
  70.1 0.7 collective-permute-start.7
  70.8 1.2 %shard_map.60.refs_1_ = f32[768,128]{1,0:T(8,128)S(1)} custom-call(f32[768,128]{1,0:T(8,128)S(1)} %get-tuple-element.48.refs_0_, f32[96,128]{1,0:T(8,128)S(1)} %get-tuple-element.49.refs_1_, f32[96,128]{1,0:T(8,128)S(1)} %get-tuple-element.50.refs_2_, f32[144,128]{1,0:T(8,128)S(1)} %get-tuple-element.34.refs_1_.refs_3_), custom_call_target="tpu_custom_call" | custom-call | flops 6291456 | bytes 6291456 | tf_op jit(solution)/shard_map/pallas_call | solution.py:465
  72.0 0.0 collective-permute-done.6.refs_4_
  72.0 0.0 collective-permute-done.7.refs_5_
  72.0 1.4 %shard_map.61 = f32[24,32,128]{2,1,0:T(8,128)} custom-call(f32[768,128]{1,0:T(8,128)S(1)} %get-tuple-element.30.refs_0_, f32[768,128]{1,0:T(8,128)S(1)} %shard_map.60.refs_1_, f32[40,8,128]{2,1,0:T(8,128)S(1)} %get-tuple-element.51.refs_2_, f32[80,128]{1,0:T(8,128)S(1)} %get-tuple-element.52.refs_3_, f32[4,8,128]{2,1,0:T(8,128)S(1)} %collective-permute-done.6.refs_4_, ...), custom_call_target="tpu_custom_call" | custom-call | tf_op jit(solution)/shard_map/pallas_call | solution.py:465
  (2 shorter events, 0.1 us)
Async XLA Ops:
  1.4 32.0 %collective-permute-start.4 = (f32[72,8,128]{2,1,0:T(8,128)S(1)}, f32[72,8,128]{2,1,0:T(8,128)S(1)}, u32[]{:S(2)}, u32[]{:S(2)}) collective-permute-start(f32[72,8,128]{2,1,0:T(8,128)S(1)} %get-tuple-element.43), channel_id=1, source_target_pairs={{0,1},{1,0},{2,3},{3,2},{4,5},{5,4},{6,7},{7,6},{8,9},{9,8},{10,11... | collective-permute-start | bytes 884744 | tf_op jit(solution)/shard_map/ppermute | solution.py:24
  4.1 29.4 %collective-permute-start.5 = (f32[72,8,128]{2,1,0:T(8,128)S(1)}, f32[72,8,128]{2,1,0:T(8,128)S(1)}, u32[]{:S(2)}, u32[]{:S(2)}) collective-permute-start(f32[72,8,128]{2,1,0:T(8,128)S(1)} %get-tuple-element.44), channel_id=1, source_target_pairs={{1,2},{2,1},{3,4},{4,3},{5,6},{6,5},{7,8},{8,7},{9,10},{10,9},{11,... | collective-permute-start | bytes 884744 | tf_op jit(solution)/shard_map/ppermute | solution.py:24
  8.4 8.6 %collective-permute-start = (f32[29,8,128]{2,1,0:T(8,128)S(1)}, f32[29,8,128]{2,1,0:T(8,128)S(1)}, u32[]{:S(2)}, u32[]{:S(2)}) collective-permute-start(f32[29,8,128]{2,1,0:T(8,128)S(1)} %get-tuple-element.32), channel_id=1, source_target_pairs={{0,1},{1,0},{2,3},{3,2},{4,5},{5,4},{6,7},{7,6},{8,9},{9,8},{10,11... | collective-permute-start | bytes 356360 | tf_op jit(solution)/shard_map/ppermute | solution.py:24
  14.1 8.8 %collective-permute-start.1 = (f32[29,8,128]{2,1,0:T(8,128)S(1)}, f32[29,8,128]{2,1,0:T(8,128)S(1)}, u32[]{:S(2)}, u32[]{:S(2)}) collective-permute-start(f32[29,8,128]{2,1,0:T(8,128)S(1)} %get-tuple-element.33), channel_id=1, source_target_pairs={{1,2},{2,1},{3,4},{4,3},{5,6},{6,5},{7,8},{8,7},{9,10},{10,9},{11,... | collective-permute-start | bytes 356360 | tf_op jit(solution)/shard_map/ppermute | solution.py:24
  23.5 9.9 %collective-permute-start.2 = (f32[6,8,128]{2,1,0:T(8,128)S(1)}, f32[6,8,128]{2,1,0:T(8,128)S(1)}, u32[]{:S(2)}, u32[]{:S(2)}) collective-permute-start(f32[6,8,128]{2,1,0:T(8,128)S(1)} %get-tuple-element.40), channel_id=1, source_target_pairs={{0,16},{16,0},{32,48},{48,32},{1,17},{17,1},{33,49},{49,33},{2,18}... | collective-permute-start | bytes 73736 | tf_op jit(solution)/shard_map/ppermute | solution.py:24
  28.8 4.6 %collective-permute-start.3 = (f32[6,8,128]{2,1,0:T(8,128)S(1)}, f32[6,8,128]{2,1,0:T(8,128)S(1)}, u32[]{:S(2)}, u32[]{:S(2)}) collective-permute-start(f32[6,8,128]{2,1,0:T(8,128)S(1)} %get-tuple-element.41), channel_id=1, source_target_pairs={{16,32},{32,16},{17,33},{33,17},{18,34},{34,18},{19,35},{35,19},{2... | collective-permute-start | bytes 73736 | tf_op jit(solution)/shard_map/ppermute | solution.py:24
  57.9 14.1 %collective-permute-start.6 = (f32[4,8,128]{2,1,0:T(8,128)S(1)}, f32[4,8,128]{2,1,0:T(8,128)S(1)}, u32[]{:S(2)}, u32[]{:S(2)}) collective-permute-start(f32[4,8,128]{2,1,0:T(8,128)S(1)} %get-tuple-element.53), channel_id=1, source_target_pairs={{0,16},{16,0},{32,48},{48,32},{1,17},{17,1},{33,49},{49,33},{2,18}... | collective-permute-start | bytes 49160 | tf_op jit(solution)/shard_map/ppermute | solution.py:24
  70.1 1.9 %collective-permute-start.7 = (f32[4,8,128]{2,1,0:T(8,128)S(1)}, f32[4,8,128]{2,1,0:T(8,128)S(1)}, u32[]{:S(2)}, u32[]{:S(2)}) collective-permute-start(f32[4,8,128]{2,1,0:T(8,128)S(1)} %get-tuple-element.54), channel_id=1, source_target_pairs={{16,32},{32,16},{17,33},{33,17},{18,34},{34,18},{19,35},{35,19},{2... | collective-permute-start | bytes 49160 | tf_op jit(solution)/shard_map/ppermute | solution.py:24
where the time goes:
time: 74.8 us; the launch traced here: 73.4 us
  starting transfers between devices  33.4 us (45%)
  blocking collectives  22.6 us (30%)
  waiting for transfers between devices  9.45 us (13%)
  Pallas kernels  7.75 us (10%)
    ppermute x8, starting transfers between devices, swap(): out.append(lax.ppermute(value, axis, pairs))  33.4 us
    all_to_all x1, blocking collectives, shards(): parts = lax.all_to_all(partial, 'mem', 0, 0)  11.3 us
    all_to_all x1, blocking collectives, shards(): increment = lax.all_to_all(jnp.broadcast_to(mine, parts.shape), 'mem', 0, 0)  11.3 us
    ppermute x8, waiting for transfers between devices, swap(): out.append(lax.ppermute(value, axis, pairs))  9.45 us
    pallas_call x7, Pallas kernels, call(): pl.pallas_call(lambda *refs: kernel(grid, *refs), compiler_params=PARAMS,...  7.75 us
  transfers between devices with their start and end apart: 8, of which 3 were waited for; matrix products, arithmetic and copies ran while one was open for 0% of the time, Pallas kernels for 4%

commit v1 on v0

--- a/solution.py
+++ b/solution.py
@@ -180,6 +180,7 @@
     far,
     outer_near,
     outer_far,
+    own_edges,
     control,
     diffusivity,
     seen,
@@ -226,6 +227,8 @@
             first = control[grid.members_at(l, r), :]
             last = control[grid.members_at(l, rows - depth + r), :]
             near[l * depth + r], far[l * depth + r] = ordered(odd, first, last)
+    for y in range(rows):
+        own_edges[y] = edges_of(grid, lambda l: control[grid.members_at(l, y), :])
     copies[4].wait()
     copies[5].wait()
     members, variables = heads.shape[:2]
@@ -240,21 +243,27 @@
                 outer_near[at], outer_far[at] = ordered(odd, first, last)
 
 
-def field_columns(grid, row_of, length, near, far, edges):
+def field_columns(grid, edges_at, length, near, far, edges):
     for start in range(0, length, grid.per):
         here = []
         for k in range(start, min(length, start + grid.per)):
-            here.append(edges_of(grid, lambda l: row_of(l, k)))
+            here.append(edges_at(k))
             edges[k] = here[-1]
         q = start // grid.per
         near[q], far[q] = ordered(is_odd("gx"), *packed(grid, here))
 
 
-def columns_kernel(grid, control, diffusivity, got_near, got_far, near, far, edges, ring, ring_edges):
+def columns_kernel(grid, own_edges, control, diffusivity, got_near, got_far, near, far, edges, ring, ring_edges):
     got = (got_near, got_far)
     odd = is_odd("gy")
-    field_columns(grid, lambda l, k: grid.wide_row(control, got, odd, l, k), grid.wide, near, far, edges)
     depth = 2 * STEPS
+
+    def edges_at(k):
+        if depth <= k < depth + grid.rows:
+            return own_edges[k - depth]
+        return edges_of(grid, lambda l: grid.wide_row(control, got, odd, l, k))
+
+    field_columns(grid, edges_at, grid.wide, near, far, edges)
     for l in range(grid.levels):
         after, before = ordered(odd, got_far[grid.levels * depth + l], got_near[grid.levels * depth + l])
         base = l * grid.wide
@@ -422,7 +431,11 @@
             at = slice((l * pairs + q) * SUBLANES, (l * pairs + q + 1) * SUBLANES)
             back_after[at, :] = totals[0][q]
             back_before[at, :] = totals[1][q]
-    field_columns(grid, lambda l, k: grid.ring_row(back, back_before, back_after, l, k), grid.ring, near, far, edges)
+
+    def edges_at(k):
+        return edges_of(grid, lambda l: grid.ring_row(back, back_before, back_after, l, k))
+
+    field_columns(grid, edges_at, grid.ring, near, far, edges)
 
 
 def adjoint_kernel(grid, control, main, edges, strip_ring, col_near, col_far, out_hbm, strip_keep, ends, out, sems):
@@ -480,14 +493,14 @@
     outer = tiles(variables * levels * members // 2)
     level_rows = shape_of(levels * rows, lanes)
     edge_rows = pltpu.VMEM((members, variables, levels, SUBLANES, lanes), perturb.dtype)
-    near, far, outer_near, outer_far, flat, flat_diff, seen, weights = call(
+    near, far, outer_near, outer_far, own_edges, flat, flat_diff, seen, weights = call(
         rows_kernel,
         in_hbm(control.reshape(count * rows, lanes)),
         in_hbm(diffusivity.reshape(levels * rows, lanes)),
         in_hbm(obs_count.reshape(levels * rows, lanes)),
         in_hbm(obs_weight),
         in_hbm(perturb),
-        out_shape=(edge, edge, outer, outer, shape_of(count * rows, lanes), level_rows, level_rows, tiles(variables)),
+        out_shape=(edge, edge, outer, outer, tiles(rows), shape_of(count * rows, lanes), level_rows, level_rows, tiles(variables)),
         in_specs=[hbm] * 5,
         scratch_shapes=[
             pltpu.VMEM(level_rows.shape, jnp.int32),
@@ -502,6 +515,7 @@
     edge = tiles(grid.wide_packs + 1)
     near, far, edges, ring, ring_edges = call(
         columns_kernel,
+        own_edges,
         flat,
         flat_diff,
         *got,

time: 74.8 us -> 74.7 us (level)
  no operation moved by 1% of the time
where the time goes in v1:
time: 74.7 us; the launch traced here: 73.4 us
  starting transfers between devices  33.4 us (45%)
  blocking collectives  22.6 us (30%)
  waiting for transfers between devices  9.45 us (13%)
  Pallas kernels  7.7 us (10%)
    ppermute x8, starting transfers between devices, swap(): out.append(lax.ppermute(value, axis, pairs))  33.4 us
    all_to_all x1, blocking collectives, shards(): parts = lax.all_to_all(partial, 'mem', 0, 0)  11.3 us
    all_to_all x1, blocking collectives, shards(): increment = lax.all_to_all(jnp.broadcast_to(mine, parts.shape), 'mem', 0, 0)  11.3 us
    ppermute x8, waiting for transfers between devices, swap(): out.append(lax.ppermute(value, axis, pairs))  9.45 us
    pallas_call x7, Pallas kernels, call(): pl.pallas_call(lambda *refs: kernel(grid, *refs), compiler_params=PARAMS,...  7.7 us
  transfers between devices with their start and end apart: 8, of which 3 were waited for; matrix products, arithmetic and copies ran while one was open for 0% of the time, Pallas kernels for 4%

profile of v1, /device:TPU:24, one launch (start us, length us, event | category | flops | bytes accessed | tf_op | source)
XLA Modules:
  0.0 73.4 jit_solution(12997978652338829629)
XLA Ops:
  0.0 1.6 %shard_map.55 = (f32[29,8,128]{2,1,0:T(8,128)S(1)}, f32[29,8,128]{2,1,0:T(8,128)S(1)}, f32[72,8,128]{2,1,0:T(8,128)S(1)}, f32[72,8,128]{2,1,0:T(8,128)S(1)}, f32...) custom-call(f32[768,128]{1,0:T(8,128)} %bitcast.4, ...), custom_call_target="tpu_custom_call" | custom-call | tf_op jit(solution)/shard_map/pallas_call | solution.py:478
  1.6 2.7 %collective-permute-start.4 = (f32[72,8,128]{2,1,0:T(8,128)S(1)}, f32[72,8,128]{2,1,0:T(8,128)S(1)}, u32[]{:S(2)}, u32[]{:S(2)}) collective-permute-start(f32[72,8,128]{2,1,0:T(8,128)S(1)} %get-tuple-element.45), channel_id=1, source_target_pairs={{0,1},{1,0},{2,3},{3,2},{4,5},{5,4},{6,7},{7,6},{8,9},{9,8},{10,11... | collective-permute-start | bytes 884744 | tf_op jit(solution)/shard_map/ppermute | solution.py:24
  4.2 4.3 %collective-permute-start.5 = (f32[72,8,128]{2,1,0:T(8,128)S(1)}, f32[72,8,128]{2,1,0:T(8,128)S(1)}, u32[]{:S(2)}, u32[]{:S(2)}) collective-permute-start(f32[72,8,128]{2,1,0:T(8,128)S(1)} %get-tuple-element.46), channel_id=1, source_target_pairs={{1,2},{2,1},{3,4},{4,3},{5,6},{6,5},{7,8},{8,7},{9,10},{10,9},{11,... | collective-permute-start | bytes 884744 | tf_op jit(solution)/shard_map/ppermute | solution.py:24
  8.6 5.7 %collective-permute-start = (f32[29,8,128]{2,1,0:T(8,128)S(1)}, f32[29,8,128]{2,1,0:T(8,128)S(1)}, u32[]{:S(2)}, u32[]{:S(2)}) collective-permute-start(f32[29,8,128]{2,1,0:T(8,128)S(1)} %get-tuple-element.34), channel_id=1, source_target_pairs={{0,1},{1,0},{2,3},{3,2},{4,5},{5,4},{6,7},{7,6},{8,9},{9,8},{10,11... | collective-permute-start | bytes 356360 | tf_op jit(solution)/shard_map/ppermute | solution.py:24
  14.3 1.9 %collective-permute-start.1 = (f32[29,8,128]{2,1,0:T(8,128)S(1)}, f32[29,8,128]{2,1,0:T(8,128)S(1)}, u32[]{:S(2)}, u32[]{:S(2)}) collective-permute-start(f32[29,8,128]{2,1,0:T(8,128)S(1)} %get-tuple-element.35), channel_id=1, source_target_pairs={{1,2},{2,1},{3,4},{4,3},{5,6},{6,5},{7,8},{8,7},{9,10},{10,9},{11,... | collective-permute-start | bytes 356360 | tf_op jit(solution)/shard_map/ppermute | solution.py:24
  16.3 0.9 %collective-permute-done.refs_3_.refs_2_.refs_6_ = f32[29,8,128]{2,1,0:T(8,128)S(1)} collective-permute-done((f32[29,8,128]{2,1,0:T(8,128)S(1)}, f32[29,8,128]{2,1,0:T(8,128)S(1)}, u32[]{:S(2)}, u32[]{:S(2)}) %collective-permute-start) | collective-permute-done | bytes 118816 | tf_op jit(solution)/shard_map/ppermute | solution.py:24
  17.1 6.0 %collective-permute-done.1.refs_4_.refs_3_.refs_7_ = f32[29,8,128]{2,1,0:T(8,128)S(1)} collective-permute-done((f32[29,8,128]{2,1,0:T(8,128)S(1)}, f32[29,8,128]{2,1,0:T(8,128)S(1)}, u32[]{:S(2)}, u32[]{:S(2)}) %collective-permute-start.1) | collective-permute-done | bytes 118816 | tf_op jit(solution)/shard_map/ppermute | solution.py:24
  23.2 0.3 shard_map.56
  23.5 5.3 %collective-permute-start.2 = (f32[6,8,128]{2,1,0:T(8,128)S(1)}, f32[6,8,128]{2,1,0:T(8,128)S(1)}, u32[]{:S(2)}, u32[]{:S(2)}) collective-permute-start(f32[6,8,128]{2,1,0:T(8,128)S(1)} %get-tuple-element.42), channel_id=1, source_target_pairs={{0,16},{16,0},{32,48},{48,32},{1,17},{17,1},{33,49},{49,33},{2,18}... | collective-permute-start | bytes 73736 | tf_op jit(solution)/shard_map/ppermute | solution.py:24
  28.8 0.7 collective-permute-start.3
  29.4 1.4 %shard_map.57 = (f32[768,128]{1,0:T(8,128)S(1)}, f32[96,128]{1,0:T(8,128)S(1)}, f32[96,128]{1,0:T(8,128)S(1)}, bf16[8,6,3,32,128]{4,3,2,1,0:T(8,128)(2,1)S(1)}) custom-call(f32[768,128]{1,0:T(8,128)S(1)} %get-tuple-element.31.refs_1_.refs_0_, f32[144,128]{1,0:T(8,128)S(1)} %get-tuple-element.36.refs_1_.refs_3_, ...), custom_call_target="tpu_custom_call" | custom-call | flops 6291456 | bytes 6291456 | tf_op jit(solution)/shard_map/pallas_call | solution.py:478
  30.8 2.5 %collective-permute-done.2.refs_5_ = f32[6,8,128]{2,1,0:T(8,128)S(1)} collective-permute-done((f32[6,8,128]{2,1,0:T(8,128)S(1)}, f32[6,8,128]{2,1,0:T(8,128)S(1)}, u32[]{:S(2)}, u32[]{:S(2)}) %collective-permute-start.2) | collective-permute-done | bytes 24608 | tf_op jit(solution)/shard_map/ppermute | solution.py:24
  33.4 0.0 collective-permute-done.3.refs_6_
  33.4 0.0 collective-permute-done.4.refs_8_.refs_4_
  33.4 0.0 collective-permute-done.5.refs_9_.refs_5_
  33.4 1.1 %shard_map.58 = (f32[8,96,128]{2,1,0:T(8,128)S(1)}, f32[80,128]{1,0:T(8,128)S(1)}) custom-call(f32[768,128]{1,0:T(8,128)S(1)} %get-tuple-element.37.refs_0_, f32[96,128]{1,0:T(8,128)S(1)} %get-tuple-element.38.refs_1_, f32[96,128]{1,0:T(8,128)S(1)} %get-tuple-element.39.refs_2_, f32[48,8,128]{2,1,0:T(8,128)S(1)} %get-tuple-element.40.refs_3_, ...), custom_call_target="tpu_custom_call" | custom-call | tf_op jit(solution)/shard_map/pallas_call | solution.py:478
  34.5 11.3 %all_to_all.10 = f32[8,96,128]{2,1,0:T(8,128)S(1)} all-to-all(f32[8,96,128]{2,1,0:T(8,128)S(1)} %get-tuple-element.47), channel_id=1, replica_groups=mesh['mem'=8,'gx'=4,'gy'=16] {'mem'}, dimensions={0} | all-to-all | bytes 786432 | tf_op jit(solution)/shard_map/all_to_all | solution.py:554
  45.8 11.3 %all_to_all.11.refs_0_ = f32[8,96,128]{2,1,0:T(8,128)S(1)} all-to-all(f32[8,96,128]{2,1,0:T(8,128)S(1)} %broadcast_in_dim.3), channel_id=1, replica_groups=mesh['mem'=8,'gx'=4,'gy'=16] {'mem'}, dimensions={0} | all-to-all | bytes 786432 | tf_op jit(solution)/shard_map/all_to_all | solution.py:556
  57.1 0.8 %shard_map.59 = (f32[768,128]{1,0:T(8,128)S(1)}, f32[96,128]{1,0:T(8,128)S(1)}, f32[96,128]{1,0:T(8,128)S(1)}, f32[40,8,128]{2,1,0:T(8,128)S(1)}, f32[4,8,128]{2,1,0:T(8,128)S(1)}, /*index=5*/f32[4,8,128]{2,1,0:T(8,128)S(1)}) custom-call(f32[8,96,128]{2,1,0:T(8,128)S(1)} %all_to_all.11.refs_0_, f32[96,128]{1,0:T(8,128)S(1)} %get-tuple-element.48.refs_1_, ...), custom_call_target="tpu_custom_call" | custom-call | tf_op jit(solution)/shard_map/pallas_call | solution.py:478
  57.9 12.2 %collective-permute-start.6 = (f32[4,8,128]{2,1,0:T(8,128)S(1)}, f32[4,8,128]{2,1,0:T(8,128)S(1)}, u32[]{:S(2)}, u32[]{:S(2)}) collective-permute-start(f32[4,8,128]{2,1,0:T(8,128)S(1)} %get-tuple-element.55), channel_id=1, source_target_pairs={{0,16},{16,0},{32,48},{48,32},{1,17},{17,1},{33,49},{49,33},{2,18}... | collective-permute-start | bytes 49160 | tf_op jit(solution)/shard_map/ppermute | solution.py:24
  70.1 0.7 collective-permute-start.7
  70.8 1.2 %shard_map.60.refs_1_ = f32[768,128]{1,0:T(8,128)S(1)} custom-call(f32[768,128]{1,0:T(8,128)S(1)} %get-tuple-element.50.refs_0_, f32[96,128]{1,0:T(8,128)S(1)} %get-tuple-element.51.refs_1_, f32[96,128]{1,0:T(8,128)S(1)} %get-tuple-element.52.refs_2_, f32[144,128]{1,0:T(8,128)S(1)} %get-tuple-element.36.refs_1_.refs_3_), custom_call_target="tpu_custom_call" | custom-call | flops 6291456 | bytes 6291456 | tf_op jit(solution)/shard_map/pallas_call | solution.py:478
  72.0 0.0 collective-permute-done.6.refs_4_
  72.0 0.0 collective-permute-done.7.refs_5_
  72.0 1.4 %shard_map.61 = f32[24,32,128]{2,1,0:T(8,128)} custom-call(f32[768,128]{1,0:T(8,128)S(1)} %get-tuple-element.31.refs_1_.refs_0_, f32[768,128]{1,0:T(8,128)S(1)} %shard_map.60.refs_1_, f32[40,8,128]{2,1,0:T(8,128)S(1)} %get-tuple-element.53.refs_2_, f32[80,128]{1,0:T(8,128)S(1)} %get-tuple-element.54.refs_3_, ...), custom_call_target="tpu_custom_call" | custom-call | tf_op jit(solution)/shard_map/pallas_call | solution.py:478
  (2 shorter events, 0.1 us)
Async XLA Ops:
  1.6 31.8 %collective-permute-start.4 = (f32[72,8,128]{2,1,0:T(8,128)S(1)}, f32[72,8,128]{2,1,0:T(8,128)S(1)}, u32[]{:S(2)}, u32[]{:S(2)}) collective-permute-start(f32[72,8,128]{2,1,0:T(8,128)S(1)} %get-tuple-element.45), channel_id=1, source_target_pairs={{0,1},{1,0},{2,3},{3,2},{4,5},{5,4},{6,7},{7,6},{8,9},{9,8},{10,11... | collective-permute-start | bytes 884744 | tf_op jit(solution)/shard_map/ppermute | solution.py:24
  4.2 29.1 %collective-permute-start.5 = (f32[72,8,128]{2,1,0:T(8,128)S(1)}, f32[72,8,128]{2,1,0:T(8,128)S(1)}, u32[]{:S(2)}, u32[]{:S(2)}) collective-permute-start(f32[72,8,128]{2,1,0:T(8,128)S(1)} %get-tuple-element.46), channel_id=1, source_target_pairs={{1,2},{2,1},{3,4},{4,3},{5,6},{6,5},{7,8},{8,7},{9,10},{10,9},{11,... | collective-permute-start | bytes 884744 | tf_op jit(solution)/shard_map/ppermute | solution.py:24
  8.6 8.6 %collective-permute-start = (f32[29,8,128]{2,1,0:T(8,128)S(1)}, f32[29,8,128]{2,1,0:T(8,128)S(1)}, u32[]{:S(2)}, u32[]{:S(2)}) collective-permute-start(f32[29,8,128]{2,1,0:T(8,128)S(1)} %get-tuple-element.34), channel_id=1, source_target_pairs={{0,1},{1,0},{2,3},{3,2},{4,5},{5,4},{6,7},{7,6},{8,9},{9,8},{10,11... | collective-permute-start | bytes 356360 | tf_op jit(solution)/shard_map/ppermute | solution.py:24
  14.3 8.8 %collective-permute-start.1 = (f32[29,8,128]{2,1,0:T(8,128)S(1)}, f32[29,8,128]{2,1,0:T(8,128)S(1)}, u32[]{:S(2)}, u32[]{:S(2)}) collective-permute-start(f32[29,8,128]{2,1,0:T(8,128)S(1)} %get-tuple-element.35), channel_id=1, source_target_pairs={{1,2},{2,1},{3,4},{4,3},{5,6},{6,5},{7,8},{8,7},{9,10},{10,9},{11,... | collective-permute-start | bytes 356360 | tf_op jit(solution)/shard_map/ppermute | solution.py:24
  23.5 9.9 %collective-permute-start.2 = (f32[6,8,128]{2,1,0:T(8,128)S(1)}, f32[6,8,128]{2,1,0:T(8,128)S(1)}, u32[]{:S(2)}, u32[]{:S(2)}) collective-permute-start(f32[6,8,128]{2,1,0:T(8,128)S(1)} %get-tuple-element.42), channel_id=1, source_target_pairs={{0,16},{16,0},{32,48},{48,32},{1,17},{17,1},{33,49},{49,33},{2,18}... | collective-permute-start | bytes 73736 | tf_op jit(solution)/shard_map/ppermute | solution.py:24
  28.8 4.6 %collective-permute-start.3 = (f32[6,8,128]{2,1,0:T(8,128)S(1)}, f32[6,8,128]{2,1,0:T(8,128)S(1)}, u32[]{:S(2)}, u32[]{:S(2)}) collective-permute-start(f32[6,8,128]{2,1,0:T(8,128)S(1)} %get-tuple-element.43), channel_id=1, source_target_pairs={{16,32},{32,16},{17,33},{33,17},{18,34},{34,18},{19,35},{35,19},{2... | collective-permute-start | bytes 73736 | tf_op jit(solution)/shard_map/ppermute | solution.py:24
  57.9 14.1 %collective-permute-start.6 = (f32[4,8,128]{2,1,0:T(8,128)S(1)}, f32[4,8,128]{2,1,0:T(8,128)S(1)}, u32[]{:S(2)}, u32[]{:S(2)}) collective-permute-start(f32[4,8,128]{2,1,0:T(8,128)S(1)} %get-tuple-element.55), channel_id=1, source_target_pairs={{0,16},{16,0},{32,48},{48,32},{1,17},{17,1},{33,49},{49,33},{2,18}... | collective-permute-start | bytes 49160 | tf_op jit(solution)/shard_map/ppermute | solution.py:24
  70.1 1.9 %collective-permute-start.7 = (f32[4,8,128]{2,1,0:T(8,128)S(1)}, f32[4,8,128]{2,1,0:T(8,128)S(1)}, u32[]{:S(2)}, u32[]{:S(2)}) collective-permute-start(f32[4,8,128]{2,1,0:T(8,128)S(1)} %get-tuple-element.56), channel_id=1, source_target_pairs={{16,32},{32,16},{17,33},{33,17},{18,34},{34,18},{19,35},{35,19},{2... | collective-permute-start | bytes 49160 | tf_op jit(solution)/shard_map/ppermute | solution.py:24
